TPU v7x, 32 devices: a whole 2x2x4 slice. The times are simulated.
32 devices in a mesh: groups: 2 (over x), gx: 16 (over z, y, core).
Axes of the slice: x: 2, y: 2, z: 4, core: 2. Of those that a mesh axis runs over, the one named last changes fastest.
Arguments:
- points: bfloat16 [32, 6, 1, 128, 512], P(('groups', 'gx')), parts along dimension 0, may hold values from -6 to 6
- order: int32 [32, 6, 1, 128], P(('groups', 'gx')), parts along dimension 0, may hold values from 0 to 127, each once within a row
- masks: int32 [32, 6, 1, 26], P(('groups', 'gx')), parts along dimension 0, may hold values 0 or 1
- counts: int32 [32, 6, 1], P('groups'), parts along dimension 0, may hold values from 1 to 128
- gain: float32 [512], replicated, may hold values from 0.5 to 1.5
- shift_bias: float32 [512], replicated, may hold values from -3 to 3
- w_qkv: bfloat16 [512, 1536], replicated, may hold values from -1.5 to 1.5
- w_out: bfloat16 [512, 512], replicated, may hold values from -0.25 to 0.25
Outputs:
- result: bfloat16 [32, 6, 1, 128, 512], P(('groups', 'gx')), parts along dimension 0
There are 2 independent parts, one for each index of `groups`. A program takes and returns all parts, laid end to end along the dimension named above; an argument that names none is the same for every part. Nothing has to cross between parts.
All inputs are finite; a program needn't handle non-finite values. No bound on the sum of `masks` on one device may be relied on, other than what follows from the above.
Results may differ from a plain program's by a relative error of at most 0.012.
Values may be sent and summed in bfloat16 or wider, within the bound.
No kernel may reach another device: no remote copies, remote signals or barrier semaphores. Data moves between devices by JAX's collectives and lax.ppermute only.
A program may use at most 128 MiB of HBM per device.

v0:
```python
import functools

import jax
import jax.numpy as jnp
from jax import lax
from jax.experimental import pallas as pl
from jax.experimental.pallas import tpu as pltpu
from jax.sharding import PartitionSpec as P


HEADS = 8
NEG = -1e30
ONES = 16
LIMIT = 24 * 1024 * 1024
BF16, F32 = jnp.bfloat16, jnp.float32


def tn(a, b):
    return lax.dot_general(a, b, (((0,), (0,)), ((), ())), preferred_element_type=F32)


def nn(a, b):
    return jnp.dot(a, b, preferred_element_type=F32)


def normalise(tiled, gain, shift):
    values = tiled.astype(F32)
    mean = jnp.mean(values, axis=-1, keepdims=True)
    var = jnp.mean((values - mean) ** 2, axis=-1, keepdims=True)
    return ((values - mean) * lax.rsqrt(var + 1e-05) * gain + shift).astype(BF16)


def select(row, raw):
    p = raw.shape[0]
    slot = lax.broadcasted_iota(jnp.int32, (p, p), 0)
    return tn((slot == row).astype(F32).astype(BF16), raw).astype(BF16)


def gather_kernel(points, order, counts, gain, shift, first, rest, places, norm, raw, rows, live, sems):
    _, by, _, p, _ = points.shape
    split = first.shape[0]
    me = lax.axis_index("gx")
    small = [
        pltpu.make_async_copy(order, rows, sems.at[by]),
        pltpu.make_async_copy(counts, live, sems.at[by + 1]),
        pltpu.make_async_copy(gain, norm.at[0:1], sems.at[by + 2]),
        pltpu.make_async_copy(shift, norm.at[1:2], sems.at[by + 3]),
    ]
    large = [
        pltpu.make_async_copy(
            points.at[0, j, 0], raw.at[j] if j < split else rest.at[j - split], sems.at[j]
        )
        for j in range(by)
    ]
    for copy in (*small[:2], *large, *small[2:]):
        copy.start()
    place = lax.broadcasted_iota(jnp.int32, (1, p), 1)
    small[0].wait()
    small[1].wait()
    picks = []
    for j in range(by):
        row = rows[0, j]
        picks.append(jnp.where(place < live[j, 0, me], row, row[:, :1]))
        if j >= split:
            places[j - split] = picks[j]
    for j in range(split):
        large[j].wait()
    for j in range(split):
        first[j] = select(picks[j], raw[j])
    for copy in (*large[split:], *small[2:]):
        copy.wait()


def rest_kernel(first, rest, places, norm, tiled, normed, second):
    split = first.shape[0]
    gain, shift = norm[0:1], norm[1:2]
    for j in range(rest.shape[0]):
        got = select(places[j], rest[j])
        tiled[split + j] = got
        got = normalise(got, gain, shift)
        second[j] = got
        normed[split + j] = got
    for j in range(split):
        got = first[j]
        tiled[j] = got
        normed[j] = normalise(got, gain, shift)


def toward_near():
    return 1 - 2 * (lax.axis_index("gx") & 1)


def column(side, b):
    index = 9 * (side + 1) + 3 * (b + 1) + 1
    if isinstance(index, int):
        return index if index < 13 else index - 1
    return jnp.where(index > 13, index - 1, index)


def list_pairs(items, masks, by, sides):
    pairs, singles = jnp.int32(0), jnp.int32(0)
    for i in range(by):
        found, last, most = jnp.int32(0), jnp.int32(0), 0
        for side, exists, j0, j1, tile0, own in sides:
            for b in (0, -1, 1):
                j = i + b
                if not j0 <= j < j1:
                    continue
                tile = tile0 + j - j0
                items[1, 2 * pairs + found] = tile
                most += 1
                if own and b == 0:
                    found = found + 1
                    last = jnp.int32(tile)
                    continue
                on = masks[0, i, 0, column(side, b)] == 1
                on = on if exists is None else on & exists
                found = found + on.astype(jnp.int32)
                last = jnp.where(on, tile, last)
        items[2, 2 * singles] = i
        items[2, 2 * singles + 1] = last
        for u in range(most // 2):
            items[0, pairs + u] = i
        pairs = pairs + (found >> 1)
        singles = singles + (found & 1)
    items[0, pairs] = 0
    for u in range(2):
        items[1, 2 * pairs + u] = 0
        items[2, 2 * singles + u] = 0
    return pairs, singles


def meetings(by, j0, j1):
    found, number = {}, 0
    for i in range(by):
        for b in (0, -1, 1):
            if j0 <= i + b < j1:
                found.setdefault(i, []).append((number, i + b))
                number += 1
    return found


def mark(plan, masks, by, side, exists, j0, j1):
    for i, ends in meetings(by, j0, j1).items():
        for number, j in ends:
            on = (masks[0, i, 0, column(side, j - i)] == 1) & exists
            plan[1, number] = on.astype(jnp.int32)
            plan[0, number] = jnp.where(on, j - j0, j1 - j0)


def attend(items, pairs, singles, keys, vals, qt, top, acc, scores, peaks):
    groups, depth, lanes = qt.shape[1:]
    hd, p = depth // 2, lanes // 2
    lead = groups // 2

    def run(count, tiles, entry):
        def score(t, g):
            i, picked = entry(t)
            rows = slice(g * depth, (g + 1) * depth)
            cols = slice(g * lanes, (g + 1) * lanes)
            peak = None
            for u, k in enumerate(picked):
                made = nn(keys[k, :, rows], qt[i, g])
                scores[u * p : (u + 1) * p, cols] = made
                peak = made if peak is None else jnp.maximum(peak, made)
            peaks[:, cols] = jnp.max(peak, axis=0, keepdims=True)

        def weigh(t, g):
            i, picked = entry(t)
            cols = slice(g * lanes, (g + 1) * lanes)
            old = top[i, :, cols]
            new = jnp.maximum(old, peaks[:, cols])
            probs = jnp.exp(scores[: tiles * p, cols] - new).astype(BF16)
            fade = jnp.exp(old - new)
            both, sums = [], []
            for h in range(2):
                rows = slice(h * (hd + ONES), (h + 1) * (hd + ONES))
                val = jnp.concatenate([vals[k, g, rows] for k in picked], axis=1)
                out = nn(val, probs[:, h * p : (h + 1) * p])
                both.append(out[:hd])
                sums.append(out[hd : hd + 8])
            return cols, new, fade, jnp.concatenate(both, axis=1), jnp.concatenate(sums, axis=1)

        def step(t, carry):
            made = []
            for g in range(0, groups, lead):
                for u in range(g, g + lead):
                    score(t + (u + lead) // groups, (u + lead) % groups)
                for u in range(g, g + lead):
                    made.append(weigh(t, u))
            i, _ = entry(t)
            for cols, new, fade, both, sums in made:
                top[i, :, cols] = new
                acc[i, :hd, cols] = acc[i, :hd, cols] * fade + both
                acc[i, hd:, cols] = acc[i, hd:, cols] * fade + sums
            return carry

        for g in range(lead):
            score(0, g)
        lax.fori_loop(0, count, step, 0)

    run(pairs, 2, lambda t: (items[0, t], (items[1, 2 * t], items[1, 2 * t + 1])))
    run(singles, 1, lambda t: (items[2, 2 * t], (items[2, 2 * t + 1],)))


def put_values(vals, tile, g0, v, live):
    p = vals.shape[3]
    hd = vals.shape[2] // 2 - ONES
    flag = jnp.broadcast_to(live.astype(F32).astype(BF16), (ONES, p))
    vt = jnp.where(live, v.T, 0.0).astype(BF16)
    for h in range(v.shape[1] // hd):
        g, r = g0 + h // 2, h % 2 * (hd + ONES)
        vals[tile, g, r : r + hd] = vt[h * hd : (h + 1) * hd]
        vals[tile, g, r + hd : r + hd + ONES] = flag


def put_blocks(tile0, x, w_all, keys, vals, lives):
    p, width = keys.shape[1:]
    wide = min(512, width)
    groups = vals.shape[1]
    for c in range(0, width, wide):
        k = nn(x, w_all[:, width + c : width + c + wide]).astype(BF16)
        v = nn(x, w_all[:, 2 * width + c : 2 * width + c + wide])
        for u, live in enumerate(lives):
            rows = slice(u * p, (u + 1) * p)
            keys[tile0 + u, :, c : c + wide] = k[rows]
            put_values(vals, tile0 + u, c * groups // width, v[rows], live)


def finish(blocks, tiled, acc, w_out, plan):
    hd = acc.shape[1] - 8
    p = tiled.shape[1]
    heads = acc.shape[2] // p
    columns = []
    for i in blocks:
        attn = acc[i, :hd] * (1.0 / acc[i, hd : hd + 1])
        attn = [attn[:, h * p : (h + 1) * p] for h in range(heads)]
        columns.append(jnp.concatenate(attn, axis=0).astype(BF16))
    mixed = tn(jnp.concatenate(columns, axis=1), w_out[...])
    place = lax.broadcasted_iota(jnp.int32, (p, 1), 0)
    made = []
    for u, i in enumerate(blocks):
        value = tiled[i].astype(F32) + mixed[u * p : (u + 1) * p]
        made.append(jnp.where(place < plan[3, 1 + i], value, 0.0).astype(BF16))
    return made


def own_kernel(
    n, split, own, masks, counts, w_qkv, w_out, qt, top, acc, w_all, w_last, plan_near, plan0, plan1, keys, vals,
    items, flags, live, scores, peaks, sems
):
    by, p, width = own.shape
    _, depth = qt.shape[1:3]
    hd = depth // 2
    copies = [
        pltpu.make_async_copy(masks, flags, sems.at[0]),
        pltpu.make_async_copy(counts, live, sems.at[1]),
        pltpu.make_async_copy(w_qkv, w_all, sems.at[2]),
        pltpu.make_async_copy(w_out, w_last, sems.at[3]),
    ]
    for copy in copies:
        copy.start()
    me = lax.axis_index("gx")
    side = toward_near()
    place = lax.broadcasted_iota(jnp.int32, (1, p), 1)
    top[...] = jnp.full_like(top, NEG)
    acc[...] = jnp.zeros_like(acc)
    copies[0].wait()
    copies[1].wait()
    pairs, singles = list_pairs(items, flags, by, [(0, None, 0, by, 0, True)])
    for plan, a, j0, j1 in ((plan_near, side, 0, by), (plan0, -side, 0, split), (plan1, -side, split, by)):
        there = (me + a >= 0) & (me + a < n)
        slab = jnp.clip(me + a, 0, n - 1)
        if plan is plan1:
            mark(plan, flags, by, a, there, j0, j1)
        else:
            plan[3, 0], plan[3, 1 + 2 * by] = list_pairs(plan, flags, by, [(a, there, j0, j1, 0, False)])
        for i in range(by):
            plan[3, 1 + i] = live[i, 0, me]
        for j in range(j0, j1):
            plan[3, 1 + by + j - j0] = live[j, 0, slab]
    zeros = jnp.zeros((hd, p), BF16)
    copies[2].wait()
    mine = own[...].reshape(by * p, width)
    wide = min(512, width)
    for c in range(0, width, wide):
        q = (nn(mine, w_all[:, c : c + wide]).astype(BF16) * BF16(1.0 / hd**0.5)).astype(F32)
        for i in range(by):
            t = q[i * p : (i + 1) * p].T.astype(BF16)
            for u in range(wide // depth):
                g, mid = c // depth + u, u * depth + hd
                qt[i, g, :hd, :p] = t[mid - hd : mid]
                qt[i, g, :hd, p:] = zeros
                qt[i, g, hd:, :p] = zeros
                qt[i, g, hd:, p:] = t[mid : mid + hd]
    put_blocks(0, mine, w_all, keys, vals, [place < live[i, 0, me] for i in range(by)])
    attend(items, pairs, singles, keys, vals, qt, top, acc, scores, peaks)
    copies[3].wait()


def far_work(rim, w_all, qt, plan, top, acc, keys, vals, scores, peaks):
    by = qt.shape[0]
    blocks, p, width = rim.shape
    place = lax.broadcasted_iota(jnp.int32, (1, p), 1)
    put_blocks(0, rim[...].reshape(blocks * p, width), w_all, keys, vals, [place < plan[3, 1 + by + j] for j in range(blocks)])
    attend(plan, plan[3, 0], plan[3, 1 + 2 * by], keys, vals, qt, top, acc, scores, peaks)


def near_kernel(rim, w_all, qt, top_in, acc_in, plan, top, acc, keys, vals, scores, peaks):
    far_work(rim, w_all, qt, plan, top, acc, keys, vals, scores, peaks)


def far_kernel(
    rim, norm, w_all, qt, top_in, acc_in, tiled, w_out, plan, top, acc, held, keys, vals, scores, peaks, nrm
):
    for j in range(rim.shape[0]):
        nrm[j] = normalise(rim[j], norm[0:1], norm[1:2])
    far_work(nrm, w_all, qt, plan, top, acc, keys, vals, scores, peaks)
    for i, value in enumerate(finish(range(held.shape[0]), tiled, acc, w_out, plan)):
        held[i] = value


def last_kernel(
    rim, w_all, qt, top, acc, tiled, w_out, held, plan, result, keys, vals, scores, out, sems
):
    by, early = tiled.shape[0], held.shape[0]
    blocks, p, width = rim.shape
    groups, depth, lanes = qt.shape[1:]
    hd = depth // 2
    copies = [pltpu.make_async_copy(held.at[i], result.at[0, i, 0], sems.at[i]) for i in range(early)]
    for copy in copies:
        copy.start()
    place = lax.broadcasted_iota(jnp.int32, (1, p), 1)
    vals[blocks] = jnp.zeros(vals.shape[1:], BF16)
    lives = [place < plan[3, 1 + by + j] for j in range(blocks)]
    put_blocks(0, rim[...].reshape(blocks * p, width), w_all, keys, vals, lives)
    met = meetings(by, by - blocks, by)
    units = [(i, g) for i in met for g in range(groups)]
    peaks, parts = {}, {}

    def score(u):
        i, g = units[u]
        rows = slice(g * depth, (g + 1) * depth)
        peak = None
        for t, (number, j) in enumerate(met[i]):
            made = nn(keys[j - (by - blocks), :, rows], qt[i, g])
            scores[u % 4, t * p : (t + 1) * p] = made
            high = jnp.where(plan[1, number] == 1, jnp.max(made, axis=0, keepdims=True), NEG)
            peak = high if peak is None else jnp.maximum(peak, high)
        peaks[u] = peak

    def weigh(u):
        i, g = units[u]
        cols = slice(g * lanes, (g + 1) * lanes)
        old = top[i, :, cols]
        new = jnp.maximum(old, peaks[u])
        probs = jnp.exp(jnp.minimum(scores[u % 4, : len(met[i]) * p] - new, 0.0)).astype(BF16)
        fade = jnp.exp(old - new)
        for h in range(2):
            rows = slice(h * (hd + ONES), (h + 1) * (hd + ONES))
            mine = slice(h * p, (h + 1) * p)
            val = jnp.concatenate([vals[plan[0, number], g, rows] for number, _ in met[i]], axis=1)
            made = nn(val, probs[:, mine])
            there = slice(g * lanes + h * p, g * lanes + (h + 1) * p)
            total = acc[i, hd : hd + 1, there] * fade[:, mine] + made[hd : hd + 1]
            value = acc[i, :hd, there] * fade[:, mine] + made[:hd]
            parts[i, 2 * g + h] = (value * (1.0 / total)).astype(BF16)

    def deliver(i):
        attn = jnp.concatenate([parts[i, h] for h in range(2 * groups)], axis=0)
        mixed = tiled[i].astype(F32) + tn(attn, w_out[...])
        rows = lax.broadcasted_iota(jnp.int32, (p, 1), 0)
        out[i - early] = jnp.where(rows < plan[3, 1 + i], mixed, 0.0).astype(BF16)
        copies.append(pltpu.make_async_copy(out.at[i - early], result.at[0, i, 0], sems.at[i]))
        copies[-1].start()

    ahead = 3
    for u in range(ahead):
        score(u)
    for u in range(len(units)):
        if u + ahead < len(units):
            score(u + ahead)
        weigh(u)
    for i in met:
        deliver(i)
    for copy in copies:
        copy.wait()


def vmem(x):
    return pltpu.with_memory_space_constraint(x, pltpu.VMEM)


def smem(x):
    return pltpu.with_memory_space_constraint(x, pltpu.SMEM)


def hbm(x):
    return pltpu.with_memory_space_constraint(x, pltpu.HBM)


def shards(n, points, order, masks, counts, gain, shift_bias, w_qkv, w_out):
    _, by, bz, p, width = points.shape
    hd = width // HEADS
    groups, depth, lanes = HEADS // 2, 2 * hd, 2 * p
    split = max(by - 2, 1)
    early = max(split - 1, 1)
    whole = pl.BlockSpec(memory_space=pltpu.VMEM)
    apart = pl.BlockSpec(memory_space=pltpu.HBM)
    words = pl.BlockSpec(memory_space=pltpu.SMEM)
    plan = pltpu.SMEM((4, 8 * by), jnp.int32)
    params = pltpu.CompilerParams(vmem_limit_bytes=LIMIT)
    points, order, masks, w_qkv, w_out = map(hbm, (points, order, masks, w_qkv, w_out))
    counts = hbm(jnp.transpose(counts, (1, 2, 0)))
    live = pltpu.SMEM(counts.shape, jnp.int32)
    flags = pltpu.SMEM(masks.shape, jnp.int32)

    first, rest, places, norm = pl.pallas_call(
        gather_kernel,
        out_shape=(
            pltpu.VMEM((split, p, width), BF16),
            pltpu.VMEM((by - split, p, width), BF16),
            pltpu.VMEM((by - split, 1, p), jnp.int32),
            pltpu.VMEM((2, width), F32),
        ),
        in_specs=[apart] * 5,
        out_specs=(whole,) * 4,
        scratch_shapes=[
            pltpu.VMEM((split, p, width), BF16),
            pltpu.VMEM(order.shape, jnp.int32),
            live,
            pltpu.SemaphoreType.DMA((by + 4,)),
        ],
        compiler_params=params,
        name="gather",
    )(points, order, counts, hbm(gain[None]), hbm(shift_bias[None]))
    tile_rest = pl.pallas_call(
        rest_kernel,
        out_shape=(
            pltpu.VMEM((by, p, width), BF16),
            pltpu.VMEM((by, p, width), BF16),
            pltpu.VMEM((by - split, p, width), BF16),
        ),
        in_specs=[whole] * 4,
        out_specs=(whole,) * 3,
        compiler_params=params,
        name="rest",
    )
    tiled, normed, second = tile_rest(vmem(first), vmem(rest), vmem(places), vmem(norm))
    near_pairs = [(i, i ^ 1) for i in range(n) if i ^ 1 < n]
    far_pairs = [(i, i + 1) for i in range(1, n - 1, 2)] + [(i + 1, i) for i in range(1, n - 1, 2)]

    def moved(value, pairs):
        return lax.ppermute(value, "gx", pairs)

    far0 = moved(first, far_pairs)
    near = moved(normed, near_pairs)
    far1 = moved(second, far_pairs)

    state = (
        pltpu.VMEM((by, 1, groups * lanes), F32),
        pltpu.VMEM((by, hd + 8, groups * lanes), F32),
    )

    def scratch(tiles):
        return [
            pltpu.VMEM((tiles, p, width), BF16),
            pltpu.VMEM((tiles, groups, depth + 2 * ONES, p), BF16),
        ]

    ahead = [
        pltpu.VMEM((2 * p, groups * lanes), F32),
        pltpu.VMEM((1, groups * lanes), F32),
    ]
    own_work = pl.pallas_call(
        functools.partial(own_kernel, n, split),
        out_shape=(
            pltpu.VMEM((by, groups, depth, lanes), BF16),
            *state,
            pltpu.VMEM(w_qkv.shape, BF16),
            pltpu.VMEM(w_out.shape, BF16),
            *(plan,) * 3,
        ),
        in_specs=[whole, apart, apart, apart, apart],
        out_specs=(whole,) * 5 + (words,) * 3,
        scratch_shapes=[*scratch(by), plan, flags, live, *ahead, pltpu.SemaphoreType.DMA((4,))],
        compiler_params=params,
        name="own",
    )
    near_work = pl.pallas_call(
        near_kernel,
        out_shape=state,
        in_specs=[*(whole,) * 5, words],
        out_specs=(whole,) * 2,
        scratch_shapes=[*scratch(by), *ahead],
        input_output_aliases={3: 0, 4: 1},
        compiler_params=params,
        name="near",
    )
    qt, top, acc, w_all, w_last, plan_near, plan0, plan1 = own_work(
        vmem(normed), masks, counts, w_qkv, w_out
    )
    top, acc = near_work(*map(vmem, (near, w_all, qt, top, acc)), smem(plan_near))
    ins = [far0, norm, w_all, qt, top, acc, tiled, w_last]
    top, acc, held = pl.pallas_call(
        far_kernel,
        out_shape=(*state, pltpu.VMEM((early, p, width), BF16)),
        in_specs=[*(whole,) * len(ins), words],
        out_specs=(whole,) * 3,
        scratch_shapes=[*scratch(split), *ahead, pltpu.VMEM((split, p, width), BF16)],
        input_output_aliases={4: 0, 5: 1},
        compiler_params=params,
        name="far",
    )(*map(vmem, ins), smem(plan0))
    ins = [far1, w_all, qt, top, acc, tiled, w_last, held]
    return pl.pallas_call(
        last_kernel,
        out_shape=pltpu.HBM((1, by, bz, p, width), BF16),
        in_specs=[*(whole,) * len(ins), words],
        out_specs=apart,
        scratch_shapes=[
            pltpu.VMEM((by - split, p, width), BF16),
            pltpu.VMEM((by - split + 1, groups, depth + 2 * ONES, p), BF16),
            pltpu.VMEM((4, 3 * p, lanes), F32),
            pltpu.VMEM((by - early, p, width), BF16),
            pltpu.SemaphoreType.DMA((by,)),
        ],
        compiler_params=params,
        name="last",
    )(*map(vmem, ins), smem(plan1))


def solution(mesh):
    placed = (
        P(("groups", "gx"), None, None, None, None),
        P(("groups", "gx"), None, None, None),
        P(("groups", "gx"), None, None, None),
        P("groups", None, None),
        P(),
        P(),
        P(),
        P(),
    )
    return jax.shard_map(
        functools.partial(shards, mesh.shape["gx"]),
        mesh=mesh,
        in_specs=placed,
        out_specs=P(("groups", "gx"), None, None, None, None),
        check_vma=False,
    )
```

profile of v0, /device:TPU:27, one launch (start us, length us, event | category | flops | bytes accessed | tf_op | source)
XLA Modules:
  0.0 28.2 jit_solution(9523369018345016085)
XLA Ops:
  0.0 1.5 %gather.1 = (bf16[4,128,512]{2,1,0:T(8,128)(2,1)S(1)}, bf16[2,128,512]{2,1,0:T(8,128)(2,1)S(1)}, s32[2,1,128]{2,1,0:T(1,128)S(1)}, f32[2,512]{1,0:T(2,128)S(1)}) custom-call(bf16[1,6,1,128,512]{4,3,2,1,0:T(8,128)(2,1)} %points.1, s32[1,6,1,128]{3,2,1,0:T(1,128)} %order.1, s32[6,1,16]{2,1,0:T(1,128)} %bitcast.3, f32[1,512]{1,0:T(1,128)} %bitcast.5, ...), custom_call_target="tpu_custom_call" | custom-call | tf_op jit(solution)/shard_map/gather/pallas_call | solution.py:418
  1.5 0.7 %rest.1 = (bf16[6,128,512]{2,1,0:T(8,128)(2,1)S(1)}, bf16[6,128,512]{2,1,0:T(8,128)(2,1)S(1)}, bf16[2,128,512]{2,1,0:T(8,128)(2,1)S(1)}) custom-call(bf16[4,128,512]{2,1,0:T(8,128)(2,1)S(1)} %get-tuple-element.25.first, bf16[2,128,512]{2,1,0:T(8,128)(2,1)S(1)} %get-tuple-element.26.rest, s32[2,1,128]{2,1,0:T(1,128)S(1)} %get-tuple-element.27.places, ...), custom_call_target="tpu_custom_call" | custom-call | tf_op jit(solution)/shard_map/rest/pallas_call | solution.py:449
  2.2 0.7 %collective-permute-start.2 = (bf16[6,128,512]{2,1,0:T(8,128)(2,1)S(1)}, bf16[6,128,512]{2,1,0:T(8,128)(2,1)S(1)}, u32[]{:S(2)}, u32[]{:S(2)}) collective-permute-start(bf16[6,128,512]{2,1,0:T(8,128)(2,1)S(1)} %get-tuple-element.30.own), channel_id=1, source_target_pairs={{0,1},{1,0},{2,3},{3,2},{4,5},{5,4},{6,7},{7,6},{8,9},{9,8},{10,11... | collective-permute-start | bytes 2359304 | tf_op jit(solution)/shard_map/ppermute | solution.py:454
  2.9 3.0 %collective-permute-start.1 = (bf16[4,128,512]{2,1,0:T(8,128)(2,1)S(1)}, bf16[4,128,512]{2,1,0:T(8,128)(2,1)S(1)}, u32[]{:S(2)}, u32[]{:S(2)}) collective-permute-start(bf16[4,128,512]{2,1,0:T(8,128)(2,1)S(1)} %get-tuple-element.25.first), channel_id=1, source_target_pairs={{1,2},{3,4},{5,6},{7,8},{9,10},{11,12},{13,14},{2,1},{4,3},{6,5},{... | collective-permute-start | bytes 1572872 | tf_op jit(solution)/shard_map/ppermute | solution.py:454
  6.0 2.5 %collective-permute-start = (bf16[2,128,512]{2,1,0:T(8,128)(2,1)S(1)}, bf16[2,128,512]{2,1,0:T(8,128)(2,1)S(1)}, u32[]{:S(2)}, u32[]{:S(2)}) collective-permute-start(bf16[2,128,512]{2,1,0:T(8,128)(2,1)S(1)} %get-tuple-element.29), channel_id=1, source_target_pairs={{1,2},{3,4},{5,6},{7,8},{9,10},{11,12},{13,14},{2,1},{4,3},{6,5},{... | collective-permute-start | bytes 786440 | tf_op jit(solution)/shard_map/ppermute | solution.py:454
  8.5 6.4 %own.1 = (bf16[6,4,128,256]{3,2,1,0:T(8,128)(2,1)S(1)}, f32[6,1,1024]{2,1,0:T(1,128)S(1)}, f32[6,72,1024]{2,1,0:T(8,128)S(1)}, bf16[512,1536]{1,0:T(8,128)(2,1)S...) custom-call(bf16[6,128,512]{2,1,0:T(8,128)(2,1)S(1)} %get-tuple-element.30., ...), custom_call_target="tpu_custom_call" | custom-call | tf_op jit(solution)/shard_map/own/pallas_call | solution.py:500
  14.9 0.0 collective-permute-done.2.rim
  14.9 3.0 %near.1 = (f32[6,1,1024]{2,1,0:T(1,128)S(1)}, f32[6,72,1024]{2,1,0:T(8,128)S(1)}) custom-call(bf16[6,128,512]{2,1,0:T(8,128)(2,1)S(1)} %collective-permute-done.2.rim, bf16[512,1536]{1,0:T(8,128)(2,1)S(1)} %get-tuple-element.31.w_all, bf16[6,4,128,256]{3,2,1,0:T(8,128)(2,1)S(1)} %get-tuple-element.32.qt, ...), custom_call_target="tpu_custom_call", output_to_operand_aliasing={{0}: (3, {}), {1}: (4, {})} | custom-call | tf_op jit(solution)/shard_map/near/pallas_call | solution.py:503
  17.9 3.9 %collective-permute-done.1.rim = bf16[4,128,512]{2,1,0:T(8,128)(2,1)S(1)} collective-permute-done((bf16[4,128,512]{2,1,0:T(8,128)(2,1)S(1)}, bf16[4,128,512]{2,1,0:T(8,128)(2,1)S(1)}, u32[]{:S(2)}, u32[]{:S(2)}) %collective-permute-start.1) | collective-permute-done | bytes 524320 | tf_op jit(solution)/shard_map/ppermute | solution.py:454
  21.9 3.7 %far.1 = (f32[6,1,1024]{2,1,0:T(1,128)S(1)}, f32[6,72,1024]{2,1,0:T(8,128)S(1)}, bf16[3,128,512]{2,1,0:T(8,128)(2,1)S(1)}) custom-call(bf16[4,128,512]{2,1,0:T(8,128)(2,1)S(1)} %collective-permute-done.1.rim, f32[2,512]{1,0:T(2,128)S(1)} %get-tuple-element.28.norm, ...), custom_call_target="tpu_custom_call", output_to_operand_aliasing={{0}: (4, {}), {1}: (5, {})} | custom-call | tf_op jit(solution)/shard_map/far/pallas_call | solution.py:505
  25.6 0.0 collective-permute-done.rim
  25.6 2.6 %last.1 = bf16[1,6,1,128,512]{4,3,2,1,0:T(8,128)(2,1)} custom-call(bf16[2,128,512]{2,1,0:T(8,128)(2,1)S(1)} %collective-permute-done.rim, bf16[512,1536]{1,0:T(8,128)(2,1)S(1)} %get-tuple-element.31.w_all, bf16[6,4,128,256]{3,2,1,0:T(8,128)(2,1)S(1)} %get-tuple-element.32.qt, f32[6,1,1024]{2,1,0:T(1,128)S(1)} %get-tuple-element.41.top, ...), custom_call_target="tpu_custom_call" | custom-call | tf_op jit(solution)/shard_map/last/pallas_call | solution.py:516
Async XLA Ops:
  2.2 12.7 %collective-permute-start.2 = (bf16[6,128,512]{2,1,0:T(8,128)(2,1)S(1)}, bf16[6,128,512]{2,1,0:T(8,128)(2,1)S(1)}, u32[]{:S(2)}, u32[]{:S(2)}) collective-permute-start(bf16[6,128,512]{2,1,0:T(8,128)(2,1)S(1)} %get-tuple-element.30.own), channel_id=1, source_target_pairs={{0,1},{1,0},{2,3},{3,2},{4,5},{5,4},{6,7},{7,6},{8,9},{9,8},{10,11... | collective-permute-start | bytes 2359304 | tf_op jit(solution)/shard_map/ppermute | solution.py:454
  2.9 18.9 %collective-permute-start.1 = (bf16[4,128,512]{2,1,0:T(8,128)(2,1)S(1)}, bf16[4,128,512]{2,1,0:T(8,128)(2,1)S(1)}, u32[]{:S(2)}, u32[]{:S(2)}) collective-permute-start(bf16[4,128,512]{2,1,0:T(8,128)(2,1)S(1)} %get-tuple-element.25.first), channel_id=1, source_target_pairs={{1,2},{3,4},{5,6},{7,8},{9,10},{11,12},{13,14},{2,1},{4,3},{6,5},{... | collective-permute-start | bytes 1572872 | tf_op jit(solution)/shard_map/ppermute | solution.py:454
  6.0 19.6 %collective-permute-start = (bf16[2,128,512]{2,1,0:T(8,128)(2,1)S(1)}, bf16[2,128,512]{2,1,0:T(8,128)(2,1)S(1)}, u32[]{:S(2)}, u32[]{:S(2)}) collective-permute-start(bf16[2,128,512]{2,1,0:T(8,128)(2,1)S(1)} %get-tuple-element.29), channel_id=1, source_target_pairs={{1,2},{3,4},{5,6},{7,8},{9,10},{11,12},{13,14},{2,1},{4,3},{6,5},{... | collective-permute-start | bytes 786440 | tf_op jit(solution)/shard_map/ppermute | solution.py:454
where the time goes:
time: 28.5 us; the launch traced here: 28.2 us
  Pallas kernels  17.9 us (63%)
  starting transfers between devices  6.29 us (22%)
  waiting for transfers between devices  3.94 us (14%)
    pallas_call x1, Pallas kernels, shards(): own_work(vmem(normed), masks, counts, w_qkv, w_out)  6.39 us
    ppermute x3, starting transfers between devices, moved(): return lax.ppermute(value, 'gx', pairs)  6.29 us
    ppermute x3, waiting for transfers between devices, moved(): return lax.ppermute(value, 'gx', pairs)  3.94 us
    pallas_call x1, Pallas kernels, shards(): pl.pallas_call(far_kernel, out_shape=(*state, pltpu.VMEM((early, p, width...  3.74 us
    pallas_call x1, Pallas kernels, shards(): near_work(*map(vmem, (near, w_all, qt, top, acc)), smem(plan_near))  3 us
    pallas_call x1, Pallas kernels, shards(): pl.pallas_call(last_kernel, out_shape=pltpu.HBM((1, by, bz, p, width), BF...  2.62 us
    pallas_call x1, Pallas kernels, shards(): pl.pallas_call(gather_kernel, out_shape=(pltpu.VMEM((split, p, width), BF...  1.53 us
    pallas_call x1, Pallas kernels, shards(): tile_rest(vmem(first), vmem(rest), vmem(places), vmem(norm))  0.65 us
  transfers between devices with their start and end apart: 3, of which 1 were waited for; matrix products, arithmetic and copies ran while one was open for 0% of the time, Pallas kernels for 47%

commit v1 on v0

--- a/solution.py
+++ b/solution.py
@@ -41,16 +41,14 @@
     split = first.shape[0]
     me = lax.axis_index("gx")
     small = [
-        pltpu.make_async_copy(order, rows, sems.at[by]),
-        pltpu.make_async_copy(counts, live, sems.at[by + 1]),
-        pltpu.make_async_copy(gain, norm.at[0:1], sems.at[by + 2]),
-        pltpu.make_async_copy(shift, norm.at[1:2], sems.at[by + 3]),
+        pltpu.make_async_copy(order, rows, sems.at[2]),
+        pltpu.make_async_copy(counts, live, sems.at[3]),
+        pltpu.make_async_copy(gain, norm.at[0:1], sems.at[4]),
+        pltpu.make_async_copy(shift, norm.at[1:2], sems.at[5]),
     ]
     large = [
-        pltpu.make_async_copy(
-            points.at[0, j, 0], raw.at[j] if j < split else rest.at[j - split], sems.at[j]
-        )
-        for j in range(by)
+        pltpu.make_async_copy(points.at[0, :split, 0], raw, sems.at[0]),
+        pltpu.make_async_copy(points.at[0, split:, 0], rest, sems.at[1]),
     ]
     for copy in (*small[:2], *large, *small[2:]):
         copy.start()
@@ -63,11 +61,10 @@
         picks.append(jnp.where(place < live[j, 0, me], row, row[:, :1]))
         if j >= split:
             places[j - split] = picks[j]
-    for j in range(split):
-        large[j].wait()
+    large[0].wait()
     for j in range(split):
         first[j] = select(picks[j], raw[j])
-    for copy in (*large[split:], *small[2:]):
+    for copy in (large[1], *small[2:]):
         copy.wait()
 
 
@@ -344,7 +341,7 @@
         peak = None
         for t, (number, j) in enumerate(met[i]):
             made = nn(keys[j - (by - blocks), :, rows], qt[i, g])
-            scores[u % 4, t * p : (t + 1) * p] = made
+            scores[u % 8, t * p : (t + 1) * p] = made
             high = jnp.where(plan[1, number] == 1, jnp.max(made, axis=0, keepdims=True), NEG)
             peak = high if peak is None else jnp.maximum(peak, high)
         peaks[u] = peak
@@ -354,7 +351,7 @@
         cols = slice(g * lanes, (g + 1) * lanes)
         old = top[i, :, cols]
         new = jnp.maximum(old, peaks[u])
-        probs = jnp.exp(jnp.minimum(scores[u % 4, : len(met[i]) * p] - new, 0.0)).astype(BF16)
+        probs = jnp.exp(jnp.minimum(scores[u % 8, : len(met[i]) * p] - new, 0.0)).astype(BF16)
         fade = jnp.exp(old - new)
         for h in range(2):
             rows = slice(h * (hd + ONES), (h + 1) * (hd + ONES))
@@ -374,7 +371,7 @@
         copies.append(pltpu.make_async_copy(out.at[i - early], result.at[0, i, 0], sems.at[i]))
         copies[-1].start()
 
-    ahead = 3
+    ahead = 6
     for u in range(ahead):
         score(u)
     for u in range(len(units)):
@@ -403,7 +400,7 @@
     _, by, bz, p, width = points.shape
     hd = width // HEADS
     groups, depth, lanes = HEADS // 2, 2 * hd, 2 * p
-    split = max(by - 2, 1)
+    split = max(by // 2, 1)
     early = max(split - 1, 1)
     whole = pl.BlockSpec(memory_space=pltpu.VMEM)
     apart = pl.BlockSpec(memory_space=pltpu.HBM)
@@ -429,7 +426,7 @@
             pltpu.VMEM((split, p, width), BF16),
             pltpu.VMEM(order.shape, jnp.int32),
             live,
-            pltpu.SemaphoreType.DMA((by + 4,)),
+            pltpu.SemaphoreType.DMA((6,)),
         ],
         compiler_params=params,
         name="gather",
@@ -521,7 +518,7 @@
         scratch_shapes=[
             pltpu.VMEM((by - split, p, width), BF16),
             pltpu.VMEM((by - split + 1, groups, depth + 2 * ONES, p), BF16),
-            pltpu.VMEM((4, 3 * p, lanes), F32),
+            pltpu.VMEM((8, 3 * p, lanes), F32),
             pltpu.VMEM((by - early, p, width), BF16),
             pltpu.SemaphoreType.DMA((by,)),
         ],

time: 28.5 us -> 28 us (0.982)
  the two profiles are of different devices: /device:TPU:27 before, /device:TPU:11 now
where the time goes in v1:
time: 28 us; the launch traced here: 27.8 us
  Pallas kernels  19.4 us (69%)
  starting transfers between devices  6.3 us (22%)
  waiting for transfers between devices  2.02 us (7%)
    pallas_call x1, Pallas kernels, shards(): own_work(vmem(normed), masks, counts, w_qkv, w_out)  6.74 us
    ppermute x3, starting transfers between devices, moved(): return lax.ppermute(value, 'gx', pairs)  6.3 us
    pallas_call x1, Pallas kernels, shards(): near_work(*map(vmem, (near, w_all, qt, top, acc)), smem(plan_near))  4.24 us
    pallas_call x1, Pallas kernels, shards(): pl.pallas_call(last_kernel, out_shape=pltpu.HBM((1, by, bz, p, width), BF...  3.28 us
    pallas_call x1, Pallas kernels, shards(): pl.pallas_call(far_kernel, out_shape=(*state, pltpu.VMEM((early, p, width...  3.13 us
    ppermute x3, waiting for transfers between devices, moved(): return lax.ppermute(value, 'gx', pairs)  2.02 us
    pallas_call x1, Pallas kernels, shards(): pl.pallas_call(gather_kernel, out_shape=(pltpu.VMEM((split, p, width), BF...  1.36 us
    pallas_call x1, Pallas kernels, shards(): tile_rest(vmem(first), vmem(rest), vmem(places), vmem(norm))  0.66 us
  transfers between devices with their start and end apart: 3, of which 2 were waited for; matrix products, arithmetic and copies ran while one was open for 0% of the time, Pallas kernels for 51%

profile of v1, /device:TPU:11, one launch (start us, length us, event | category | flops | bytes accessed | tf_op | source)
XLA Modules:
  0.0 27.8 jit_solution(6133739380877155123)
XLA Ops:
  0.0 1.4 %gather.1 = (bf16[3,128,512]{2,1,0:T(8,128)(2,1)S(1)}, bf16[3,128,512]{2,1,0:T(8,128)(2,1)S(1)}, s32[3,1,128]{2,1,0:T(1,128)S(1)}, f32[2,512]{1,0:T(2,128)S(1)}) custom-call(bf16[1,6,1,128,512]{4,3,2,1,0:T(8,128)(2,1)} %points.1, s32[1,6,1,128]{3,2,1,0:T(1,128)} %order.1, s32[6,1,16]{2,1,0:T(1,128)} %bitcast.3, f32[1,512]{1,0:T(1,128)} %bitcast.5, ...), custom_call_target="tpu_custom_call" | custom-call | tf_op jit(solution)/shard_map/gather/pallas_call | solution.py:415
  1.4 0.7 %rest.1 = (bf16[6,128,512]{2,1,0:T(8,128)(2,1)S(1)}, bf16[6,128,512]{2,1,0:T(8,128)(2,1)S(1)}, bf16[3,128,512]{2,1,0:T(8,128)(2,1)S(1)}) custom-call(bf16[3,128,512]{2,1,0:T(8,128)(2,1)S(1)} %get-tuple-element.25.first, bf16[3,128,512]{2,1,0:T(8,128)(2,1)S(1)} %get-tuple-element.26.rest, s32[3,1,128]{2,1,0:T(1,128)S(1)} %get-tuple-element.27.places, ...), custom_call_target="tpu_custom_call" | custom-call | tf_op jit(solution)/shard_map/rest/pallas_call | solution.py:446
  2.0 0.7 %collective-permute-start.2 = (bf16[6,128,512]{2,1,0:T(8,128)(2,1)S(1)}, bf16[6,128,512]{2,1,0:T(8,128)(2,1)S(1)}, u32[]{:S(2)}, u32[]{:S(2)}) collective-permute-start(bf16[6,128,512]{2,1,0:T(8,128)(2,1)S(1)} %get-tuple-element.30.own), channel_id=1, source_target_pairs={{0,1},{1,0},{2,3},{3,2},{4,5},{5,4},{6,7},{7,6},{8,9},{9,8},{10,11... | collective-permute-start | bytes 2359304 | tf_op jit(solution)/shard_map/ppermute | solution.py:451
  2.8 3.0 %collective-permute-start.1 = (bf16[3,128,512]{2,1,0:T(8,128)(2,1)S(1)}, bf16[3,128,512]{2,1,0:T(8,128)(2,1)S(1)}, u32[]{:S(2)}, u32[]{:S(2)}) collective-permute-start(bf16[3,128,512]{2,1,0:T(8,128)(2,1)S(1)} %get-tuple-element.25.first), channel_id=1, source_target_pairs={{1,2},{3,4},{5,6},{7,8},{9,10},{11,12},{13,14},{2,1},{4,3},{6,5},{... | collective-permute-start | bytes 1179656 | tf_op jit(solution)/shard_map/ppermute | solution.py:451
  5.8 2.5 %collective-permute-start = (bf16[3,128,512]{2,1,0:T(8,128)(2,1)S(1)}, bf16[3,128,512]{2,1,0:T(8,128)(2,1)S(1)}, u32[]{:S(2)}, u32[]{:S(2)}) collective-permute-start(bf16[3,128,512]{2,1,0:T(8,128)(2,1)S(1)} %get-tuple-element.29), channel_id=1, source_target_pairs={{1,2},{3,4},{5,6},{7,8},{9,10},{11,12},{13,14},{2,1},{4,3},{6,5},{... | collective-permute-start | bytes 1179656 | tf_op jit(solution)/shard_map/ppermute | solution.py:451
  8.4 6.7 %own.1 = (bf16[6,4,128,256]{3,2,1,0:T(8,128)(2,1)S(1)}, f32[6,1,1024]{2,1,0:T(1,128)S(1)}, f32[6,72,1024]{2,1,0:T(8,128)S(1)}, bf16[512,1536]{1,0:T(8,128)(2,1)S...) custom-call(bf16[6,128,512]{2,1,0:T(8,128)(2,1)S(1)} %get-tuple-element.30., ...), custom_call_target="tpu_custom_call" | custom-call | tf_op jit(solution)/shard_map/own/pallas_call | solution.py:497
  15.1 0.0 collective-permute-done.2.rim
  15.1 4.2 %near.1 = (f32[6,1,1024]{2,1,0:T(1,128)S(1)}, f32[6,72,1024]{2,1,0:T(8,128)S(1)}) custom-call(bf16[6,128,512]{2,1,0:T(8,128)(2,1)S(1)} %collective-permute-done.2.rim, bf16[512,1536]{1,0:T(8,128)(2,1)S(1)} %get-tuple-element.31.w_all, bf16[6,4,128,256]{3,2,1,0:T(8,128)(2,1)S(1)} %get-tuple-element.32.qt, ...), custom_call_target="tpu_custom_call", output_to_operand_aliasing={{0}: (3, {}), {1}: (4, {})} | custom-call | tf_op jit(solution)/shard_map/near/pallas_call | solution.py:500
  19.4 0.9 %collective-permute-done.1.rim = bf16[3,128,512]{2,1,0:T(8,128)(2,1)S(1)} collective-permute-done((bf16[3,128,512]{2,1,0:T(8,128)(2,1)S(1)}, bf16[3,128,512]{2,1,0:T(8,128)(2,1)S(1)}, u32[]{:S(2)}, u32[]{:S(2)}) %collective-permute-start.1) | collective-permute-done | bytes 393248 | tf_op jit(solution)/shard_map/ppermute | solution.py:451
  20.3 3.1 %far.1 = (f32[6,1,1024]{2,1,0:T(1,128)S(1)}, f32[6,72,1024]{2,1,0:T(8,128)S(1)}, bf16[2,128,512]{2,1,0:T(8,128)(2,1)S(1)}) custom-call(bf16[3,128,512]{2,1,0:T(8,128)(2,1)S(1)} %collective-permute-done.1.rim, f32[2,512]{1,0:T(2,128)S(1)} %get-tuple-element.28.norm, ...), custom_call_target="tpu_custom_call", output_to_operand_aliasing={{0}: (4, {}), {1}: (5, {})} | custom-call | tf_op jit(solution)/shard_map/far/pallas_call | solution.py:502
  23.4 1.1 %collective-permute-done.rim = bf16[3,128,512]{2,1,0:T(8,128)(2,1)S(1)} collective-permute-done((bf16[3,128,512]{2,1,0:T(8,128)(2,1)S(1)}, bf16[3,128,512]{2,1,0:T(8,128)(2,1)S(1)}, u32[]{:S(2)}, u32[]{:S(2)}) %collective-permute-start) | collective-permute-done | bytes 393248 | tf_op jit(solution)/shard_map/ppermute | solution.py:451
  24.5 3.3 %last.1 = bf16[1,6,1,128,512]{4,3,2,1,0:T(8,128)(2,1)} custom-call(bf16[3,128,512]{2,1,0:T(8,128)(2,1)S(1)} %collective-permute-done.rim, bf16[512,1536]{1,0:T(8,128)(2,1)S(1)} %get-tuple-element.31.w_all, bf16[6,4,128,256]{3,2,1,0:T(8,128)(2,1)S(1)} %get-tuple-element.32.qt, f32[6,1,1024]{2,1,0:T(1,128)S(1)} %get-tuple-element.41.top, ...), custom_call_target="tpu_custom_call" | custom-call | tf_op jit(solution)/shard_map/last/pallas_call | solution.py:513
Async XLA Ops:
  2.0 13.1 %collective-permute-start.2 = (bf16[6,128,512]{2,1,0:T(8,128)(2,1)S(1)}, bf16[6,128,512]{2,1,0:T(8,128)(2,1)S(1)}, u32[]{:S(2)}, u32[]{:S(2)}) collective-permute-start(bf16[6,128,512]{2,1,0:T(8,128)(2,1)S(1)} %get-tuple-element.30.own), channel_id=1, source_target_pairs={{0,1},{1,0},{2,3},{3,2},{4,5},{5,4},{6,7},{7,6},{8,9},{9,8},{10,11... | collective-permute-start | bytes 2359304 | tf_op jit(solution)/shard_map/ppermute | solution.py:451
  2.8 17.5 %collective-permute-start.1 = (bf16[3,128,512]{2,1,0:T(8,128)(2,1)S(1)}, bf16[3,128,512]{2,1,0:T(8,128)(2,1)S(1)}, u32[]{:S(2)}, u32[]{:S(2)}) collective-permute-start(bf16[3,128,512]{2,1,0:T(8,128)(2,1)S(1)} %get-tuple-element.25.first), channel_id=1, source_target_pairs={{1,2},{3,4},{5,6},{7,8},{9,10},{11,12},{13,14},{2,1},{4,3},{6,5},{... | collective-permute-start | bytes 1179656 | tf_op jit(solution)/shard_map/ppermute | solution.py:451
  5.8 18.7 %collective-permute-start = (bf16[3,128,512]{2,1,0:T(8,128)(2,1)S(1)}, bf16[3,128,512]{2,1,0:T(8,128)(2,1)S(1)}, u32[]{:S(2)}, u32[]{:S(2)}) collective-permute-start(bf16[3,128,512]{2,1,0:T(8,128)(2,1)S(1)} %get-tuple-element.29), channel_id=1, source_target_pairs={{1,2},{3,4},{5,6},{7,8},{9,10},{11,12},{13,14},{2,1},{4,3},{6,5},{... | collective-permute-start | bytes 1179656 | tf_op jit(solution)/shard_map/ppermute | solution.py:451

commit v2 on v1

--- a/solution.py
+++ b/solution.py
@@ -50,7 +50,7 @@
         pltpu.make_async_copy(points.at[0, :split, 0], raw, sems.at[0]),
         pltpu.make_async_copy(points.at[0, split:, 0], rest, sems.at[1]),
     ]
-    for copy in (*small[:2], *large, *small[2:]):
+    for copy in (large[0], *small[:2], large[1], *small[2:]):
         copy.start()
     place = lax.broadcasted_iota(jnp.int32, (1, p), 1)
     small[0].wait()
@@ -324,9 +324,8 @@
     blocks, p, width = rim.shape
     groups, depth, lanes = qt.shape[1:]
     hd = depth // 2
-    copies = [pltpu.make_async_copy(held.at[i], result.at[0, i, 0], sems.at[i]) for i in range(early)]
-    for copy in copies:
-        copy.start()
+    copies = [pltpu.make_async_copy(held, result.at[0, :early, 0], sems.at[0])]
+    copies[0].start()
     place = lax.broadcasted_iota(jnp.int32, (1, p), 1)
     vals[blocks] = jnp.zeros(vals.shape[1:], BF16)
     lives = [place < plan[3, 1 + by + j] for j in range(blocks)]
@@ -363,13 +362,15 @@
             value = acc[i, :hd, there] * fade[:, mine] + made[:hd]
             parts[i, 2 * g + h] = (value * (1.0 / total)).astype(BF16)
 
-    def deliver(i):
-        attn = jnp.concatenate([parts[i, h] for h in range(2 * groups)], axis=0)
-        mixed = tiled[i].astype(F32) + tn(attn, w_out[...])
+    def deliver(some):
+        columns = [jnp.concatenate([parts[i, h] for h in range(2 * groups)], axis=0) for i in some]
+        mixed = tn(jnp.concatenate(columns, axis=1), w_out[...])
         rows = lax.broadcasted_iota(jnp.int32, (p, 1), 0)
-        out[i - early] = jnp.where(rows < plan[3, 1 + i], mixed, 0.0).astype(BF16)
-        copies.append(pltpu.make_async_copy(out.at[i - early], result.at[0, i, 0], sems.at[i]))
-        copies[-1].start()
+        for u, i in enumerate(some):
+            value = tiled[i].astype(F32) + mixed[u * p : (u + 1) * p]
+            out[i - early] = jnp.where(rows < plan[3, 1 + i], value, 0.0).astype(BF16)
+            copies.append(pltpu.make_async_copy(out.at[i - early], result.at[0, i, 0], sems.at[i]))
+            copies[-1].start()
 
     ahead = 6
     for u in range(ahead):
@@ -378,8 +379,9 @@
         if u + ahead < len(units):
             score(u + ahead)
         weigh(u)
-    for i in met:
-        deliver(i)
+    some = list(met)
+    for c in range(0, len(some), 2):
+        deliver(some[c : c + 2])
     for copy in copies:
         copy.wait()
 

time: 28 us -> 28 us (level)
  the two profiles are of different devices: /device:TPU:11 before, /device:TPU:19 now
where the time goes in v2:
time: 28 us; the launch traced here: 27.8 us
  Pallas kernels  18.3 us (65%)
  starting transfers between devices  6.3 us (22%)
  waiting for transfers between devices  3.15 us (11%)
    ppermute x3, starting transfers between devices, moved(): return lax.ppermute(value, 'gx', pairs)  6.3 us
    pallas_call x1, Pallas kernels, shards(): own_work(vmem(normed), masks, counts, w_qkv, w_out)  5.92 us
    pallas_call x1, Pallas kernels, shards(): near_work(*map(vmem, (near, w_all, qt, top, acc)), smem(plan_near))  4.34 us
    pallas_call x1, Pallas kernels, shards(): pl.pallas_call(last_kernel, out_shape=pltpu.HBM((1, by, bz, p, width), BF...  3.28 us
    ppermute x3, waiting for transfers between devices, moved(): return lax.ppermute(value, 'gx', pairs)  3.15 us
    pallas_call x1, Pallas kernels, shards(): pl.pallas_call(far_kernel, out_shape=(*state, pltpu.VMEM((early, p, width...  2.72 us
    pallas_call x1, Pallas kernels, shards(): pl.pallas_call(gather_kernel, out_shape=(pltpu.VMEM((split, p, width), BF...  1.34 us
    pallas_call x1, Pallas kernels, shards(): tile_rest(vmem(first), vmem(rest), vmem(places), vmem(norm))  0.66 us
  transfers between devices with their start and end apart: 3, of which 2 were waited for; matrix products, arithmetic and copies ran while one was open for 0% of the time, Pallas kernels for 47%

profile of v2, /device:TPU:19, one launch (start us, length us, event | category | flops | bytes accessed | tf_op | source)
XLA Modules:
  0.0 27.8 jit_solution(13453340515528658838)
XLA Ops:
  0.0 1.3 %gather.1 = (bf16[3,128,512]{2,1,0:T(8,128)(2,1)S(1)}, bf16[3,128,512]{2,1,0:T(8,128)(2,1)S(1)}, s32[3,1,128]{2,1,0:T(1,128)S(1)}, f32[2,512]{1,0:T(2,128)S(1)}) custom-call(bf16[1,6,1,128,512]{4,3,2,1,0:T(8,128)(2,1)} %points.1, s32[1,6,1,128]{3,2,1,0:T(1,128)} %order.1, s32[6,1,16]{2,1,0:T(1,128)} %bitcast.3, f32[1,512]{1,0:T(1,128)} %bitcast.5, ...), custom_call_target="tpu_custom_call" | custom-call | tf_op jit(solution)/shard_map/gather/pallas_call | solution.py:417
  1.4 0.7 %rest.1 = (bf16[6,128,512]{2,1,0:T(8,128)(2,1)S(1)}, bf16[6,128,512]{2,1,0:T(8,128)(2,1)S(1)}, bf16[3,128,512]{2,1,0:T(8,128)(2,1)S(1)}) custom-call(bf16[3,128,512]{2,1,0:T(8,128)(2,1)S(1)} %get-tuple-element.25.first, bf16[3,128,512]{2,1,0:T(8,128)(2,1)S(1)} %get-tuple-element.26.rest, s32[3,1,128]{2,1,0:T(1,128)S(1)} %get-tuple-element.27.places, ...), custom_call_target="tpu_custom_call" | custom-call | tf_op jit(solution)/shard_map/rest/pallas_call | solution.py:448
  2.0 0.7 %collective-permute-start.2 = (bf16[6,128,512]{2,1,0:T(8,128)(2,1)S(1)}, bf16[6,128,512]{2,1,0:T(8,128)(2,1)S(1)}, u32[]{:S(2)}, u32[]{:S(2)}) collective-permute-start(bf16[6,128,512]{2,1,0:T(8,128)(2,1)S(1)} %get-tuple-element.30.own), channel_id=1, source_target_pairs={{0,1},{1,0},{2,3},{3,2},{4,5},{5,4},{6,7},{7,6},{8,9},{9,8},{10,11... | collective-permute-start | bytes 2359304 | tf_op jit(solution)/shard_map/ppermute | solution.py:453
  2.8 3.0 %collective-permute-start.1 = (bf16[3,128,512]{2,1,0:T(8,128)(2,1)S(1)}, bf16[3,128,512]{2,1,0:T(8,128)(2,1)S(1)}, u32[]{:S(2)}, u32[]{:S(2)}) collective-permute-start(bf16[3,128,512]{2,1,0:T(8,128)(2,1)S(1)} %get-tuple-element.25.first), channel_id=1, source_target_pairs={{1,2},{3,4},{5,6},{7,8},{9,10},{11,12},{13,14},{2,1},{4,3},{6,5},{... | collective-permute-start | bytes 1179656 | tf_op jit(solution)/shard_map/ppermute | solution.py:453
  5.8 2.5 %collective-permute-start = (bf16[3,128,512]{2,1,0:T(8,128)(2,1)S(1)}, bf16[3,128,512]{2,1,0:T(8,128)(2,1)S(1)}, u32[]{:S(2)}, u32[]{:S(2)}) collective-permute-start(bf16[3,128,512]{2,1,0:T(8,128)(2,1)S(1)} %get-tuple-element.29), channel_id=1, source_target_pairs={{1,2},{3,4},{5,6},{7,8},{9,10},{11,12},{13,14},{2,1},{4,3},{6,5},{... | collective-permute-start | bytes 1179656 | tf_op jit(solution)/shard_map/ppermute | solution.py:453
  8.3 5.9 %own.1 = (bf16[6,4,128,256]{3,2,1,0:T(8,128)(2,1)S(1)}, f32[6,1,1024]{2,1,0:T(1,128)S(1)}, f32[6,72,1024]{2,1,0:T(8,128)S(1)}, bf16[512,1536]{1,0:T(8,128)(2,1)S...) custom-call(bf16[6,128,512]{2,1,0:T(8,128)(2,1)S(1)} %get-tuple-element.30., ...), custom_call_target="tpu_custom_call" | custom-call | tf_op jit(solution)/shard_map/own/pallas_call | solution.py:499
  14.3 0.0 collective-permute-done.2.rim
  14.3 4.3 %near.1 = (f32[6,1,1024]{2,1,0:T(1,128)S(1)}, f32[6,72,1024]{2,1,0:T(8,128)S(1)}) custom-call(bf16[6,128,512]{2,1,0:T(8,128)(2,1)S(1)} %collective-permute-done.2.rim, bf16[512,1536]{1,0:T(8,128)(2,1)S(1)} %get-tuple-element.31.w_all, bf16[6,4,128,256]{3,2,1,0:T(8,128)(2,1)S(1)} %get-tuple-element.32.qt, ...), custom_call_target="tpu_custom_call", output_to_operand_aliasing={{0}: (3, {}), {1}: (4, {})} | custom-call | tf_op jit(solution)/shard_map/near/pallas_call | solution.py:502
  18.6 1.7 %collective-permute-done.1.rim = bf16[3,128,512]{2,1,0:T(8,128)(2,1)S(1)} collective-permute-done((bf16[3,128,512]{2,1,0:T(8,128)(2,1)S(1)}, bf16[3,128,512]{2,1,0:T(8,128)(2,1)S(1)}, u32[]{:S(2)}, u32[]{:S(2)}) %collective-permute-start.1) | collective-permute-done | bytes 393248 | tf_op jit(solution)/shard_map/ppermute | solution.py:453
  20.3 2.7 %far.1 = (f32[6,1,1024]{2,1,0:T(1,128)S(1)}, f32[6,72,1024]{2,1,0:T(8,128)S(1)}, bf16[2,128,512]{2,1,0:T(8,128)(2,1)S(1)}) custom-call(bf16[3,128,512]{2,1,0:T(8,128)(2,1)S(1)} %collective-permute-done.1.rim, f32[2,512]{1,0:T(2,128)S(1)} %get-tuple-element.28.norm, ...), custom_call_target="tpu_custom_call", output_to_operand_aliasing={{0}: (4, {}), {1}: (5, {})} | custom-call | tf_op jit(solution)/shard_map/far/pallas_call | solution.py:504
  23.0 1.5 %collective-permute-done.rim = bf16[3,128,512]{2,1,0:T(8,128)(2,1)S(1)} collective-permute-done((bf16[3,128,512]{2,1,0:T(8,128)(2,1)S(1)}, bf16[3,128,512]{2,1,0:T(8,128)(2,1)S(1)}, u32[]{:S(2)}, u32[]{:S(2)}) %collective-permute-start) | collective-permute-done | bytes 393248 | tf_op jit(solution)/shard_map/ppermute | solution.py:453
  24.5 3.3 %last.1 = bf16[1,6,1,128,512]{4,3,2,1,0:T(8,128)(2,1)} custom-call(bf16[3,128,512]{2,1,0:T(8,128)(2,1)S(1)} %collective-permute-done.rim, bf16[512,1536]{1,0:T(8,128)(2,1)S(1)} %get-tuple-element.31.w_all, bf16[6,4,128,256]{3,2,1,0:T(8,128)(2,1)S(1)} %get-tuple-element.32.qt, f32[6,1,1024]{2,1,0:T(1,128)S(1)} %get-tuple-element.41.top, ...), custom_call_target="tpu_custom_call" | custom-call | tf_op jit(solution)/shard_map/last/pallas_call | solution.py:515
Async XLA Ops:
  2.0 12.2 %collective-permute-start.2 = (bf16[6,128,512]{2,1,0:T(8,128)(2,1)S(1)}, bf16[6,128,512]{2,1,0:T(8,128)(2,1)S(1)}, u32[]{:S(2)}, u32[]{:S(2)}) collective-permute-start(bf16[6,128,512]{2,1,0:T(8,128)(2,1)S(1)} %get-tuple-element.30.own), channel_id=1, source_target_pairs={{0,1},{1,0},{2,3},{3,2},{4,5},{5,4},{6,7},{7,6},{8,9},{9,8},{10,11... | collective-permute-start | bytes 2359304 | tf_op jit(solution)/shard_map/ppermute | solution.py:453
  2.8 17.5 %collective-permute-start.1 = (bf16[3,128,512]{2,1,0:T(8,128)(2,1)S(1)}, bf16[3,128,512]{2,1,0:T(8,128)(2,1)S(1)}, u32[]{:S(2)}, u32[]{:S(2)}) collective-permute-start(bf16[3,128,512]{2,1,0:T(8,128)(2,1)S(1)} %get-tuple-element.25.first), channel_id=1, source_target_pairs={{1,2},{3,4},{5,6},{7,8},{9,10},{11,12},{13,14},{2,1},{4,3},{6,5},{... | collective-permute-start | bytes 1179656 | tf_op jit(solution)/shard_map/ppermute | solution.py:453
  5.8 18.7 %collective-permute-start = (bf16[3,128,512]{2,1,0:T(8,128)(2,1)S(1)}, bf16[3,128,512]{2,1,0:T(8,128)(2,1)S(1)}, u32[]{:S(2)}, u32[]{:S(2)}) collective-permute-start(bf16[3,128,512]{2,1,0:T(8,128)(2,1)S(1)} %get-tuple-element.29), channel_id=1, source_target_pairs={{1,2},{3,4},{5,6},{7,8},{9,10},{11,12},{13,14},{2,1},{4,3},{6,5},{... | collective-permute-start | bytes 1179656 | tf_op jit(solution)/shard_map/ppermute | solution.py:453
